TPU v7x, 128 devices: a whole 4x4x4 slice. The times are simulated.
128 devices in a mesh: row: 16 (over x, z_hi, core), col: 8 (over y, z_lo).
Axes of the slice: x: 4, y: 4, z: 4 (z_hi: 2, z_lo: 2; z = z_hi * 2 + z_lo), core: 2. Of those that a mesh axis runs over, the one named last changes fastest.
Arguments:
- features: bfloat16 [1024, 128], P(('row', 'col')), may hold values from -6 to 6
- row_weight: bfloat16 [128, 32], replicated, may hold values from -0.5 to 0.5
- col_weight: bfloat16 [128, 32], replicated, may hold values from -0.5 to 0.5
- conv_weight: bfloat16 [2, 9, 64, 64], replicated, may hold values from -0.25 to 0.25
- conv_bias: float32 [2, 64], replicated, may hold values from -3 to 3
- dilations: int32 [2], replicated, may hold values from 1 to 4, as said below
Outputs:
- pair_map: bfloat16 [64, 1024, 1024], P(None, 'row', 'col')
Inputs may be any that keep to these rules, and one draw needn't show every extreme that they name: `dilations`: one dilation a layer; at least one layer uses exactly 4.
All inputs are finite; a program needn't handle non-finite values.
Results may differ from a plain program's by a relative error of at most 0.008.
Values may be sent and summed in bfloat16 or wider, within the bound.
A program may use at most 64 MiB of HBM per device.

v0:
```python
import jax
import jax.numpy as jnp
from jax import lax
from jax.sharding import PartitionSpec as P

MAXDIL = 4


def with_halo(block, sides, width):
    for axis, dim in sides:
        count = lax.axis_size(axis)
        forward = [(i, i + 1) for i in range(count - 1)]
        backward = [(target, source) for source, target in forward]
        low = lax.ppermute(
            lax.slice_in_dim(block, block.shape[dim] - width, None, axis=dim), axis, forward
        )
        high = lax.ppermute(lax.slice_in_dim(block, 0, width, axis=dim), axis, backward)
        block = jnp.concatenate([low, block, high], axis=dim)
    return block


def tap_groups(padded, weights, dilation):
    out_channels = weights.shape[1]
    in_channels = weights.shape[2]
    row_count = padded.shape[1] - 2 * MAXDIL
    col_count = padded.shape[2] - 2 * MAXDIL
    zero_index = jnp.zeros((), jnp.int32)
    dilation = jnp.asarray(dilation)
    summed = jnp.zeros((out_channels, row_count * col_count), jnp.float32)
    for group_index in range(3):
        outer_step = group_index - 1
        pieces = []
        for inner_index in range(3):
            inner_step = inner_index - 1
            row_step, col_step = (outer_step, inner_step)
            row_index = MAXDIL + row_step * dilation
            col_index = MAXDIL + col_step * dilation
            pieces.append(
                lax.dynamic_slice(
                    padded, (zero_index, row_index, col_index), (in_channels, row_count, col_count)
                )
            )
        stacked = jnp.concatenate(pieces, axis=0).reshape(3 * in_channels, row_count * col_count)
        group_weight = jnp.transpose(
            weights[3 * group_index : 3 * group_index + 3], (1, 0, 2)
        ).reshape(out_channels, 3 * in_channels)
        summed = summed + jnp.dot(group_weight, stacked, preferred_element_type=jnp.float32)
    return summed.reshape(out_channels, row_count, col_count)


def finish_layer(pair_now, shift_bias, summed):
    mixed_map = (pair_now.astype(jnp.float32) + shift_bias[:, None, None] + summed).astype(
        jnp.bfloat16
    )
    return lax.optimization_barrier(mixed_map)


def average_pair(mixed_map, mirrored):
    return (0.5 * (mixed_map.astype(jnp.float32) + mirrored.astype(jnp.float32))).astype(
        jnp.bfloat16
    )


def inside_mask(start, count, bins_total):
    places = jnp.arange(count + 2 * MAXDIL) + start - MAXDIL
    return ((places >= 0) & (places < bins_total)).astype(jnp.bfloat16)


def local_start(row_all, col_all, row_start, row_size, col_start, col_size):
    bins_total = row_all.shape[0]
    row_padded = jnp.pad(row_all, ((MAXDIL, MAXDIL), (0, 0)))
    col_padded = jnp.pad(col_all, ((MAXDIL, MAXDIL), (0, 0)))
    row_mask = inside_mask(row_start, row_size, bins_total)
    col_mask = inside_mask(col_start, col_size, bins_total)
    rows_here = lax.dynamic_slice_in_dim(row_padded, row_start, row_size + 2 * MAXDIL, 0)
    cols_here = lax.dynamic_slice_in_dim(col_padded, col_start, col_size + 2 * MAXDIL, 0)
    pair_ext = jnp.concatenate(
        [
            rows_here.T[:, :, None] * col_mask[None, None, :],
            cols_here.T[:, None, :] * row_mask[None, :, None],
        ],
        axis=0,
    )
    rows_across = lax.dynamic_slice_in_dim(row_padded, col_start, col_size + 2 * MAXDIL, 0)
    cols_across = lax.dynamic_slice_in_dim(col_padded, row_start, row_size + 2 * MAXDIL, 0)
    mirror_ext = jnp.concatenate(
        [
            rows_across.T[:, None, :] * row_mask[None, :, None],
            cols_across.T[:, :, None] * col_mask[None, None, :],
        ],
        axis=0,
    )
    return (pair_ext, mirror_ext)


def interior(extended):
    return extended[:, MAXDIL : extended.shape[1] - MAXDIL, MAXDIL : extended.shape[2] - MAXDIL]


def grid_start(row_all, col_all):
    bins_total = row_all.shape[0]
    row_size = bins_total // lax.axis_size("row")
    col_size = bins_total // lax.axis_size("col")
    return local_start(
        row_all,
        col_all,
        lax.axis_index("row") * row_size,
        row_size,
        lax.axis_index("col") * col_size,
        col_size,
    )


def grid_layer(pair_now, padded, layer_weight, shift_bias, dilation):
    if padded is None:
        padded = with_halo(jax.nn.relu(pair_now), (("row", 1), ("col", 2)), MAXDIL)
    summed = tap_groups(padded, layer_weight, dilation)
    mixed_map = finish_layer(pair_now, shift_bias, summed)
    strips = lax.all_to_all(mixed_map, "col", split_axis=1, concat_axis=2, tiled=True)
    turned = lax.all_to_all(
        jnp.swapaxes(strips, 1, 2), ("row", "col"), split_axis=1, concat_axis=2, tiled=True
    )
    mirrored = lax.all_to_all(turned, "col", split_axis=2, concat_axis=1, tiled=True)
    return average_pair(mixed_map, mirrored)


def grid_plan(row_all, col_all, conv_weight, conv_bias, dilations):
    pair_ext, mirror_ext = grid_start(row_all, col_all)
    pair_now = grid_layer(
        interior(pair_ext), jax.nn.relu(pair_ext), conv_weight[0], conv_bias[0], dilations[0]
    )
    pair_now = grid_layer(pair_now, None, conv_weight[1], conv_bias[1], dilations[1])
    return pair_now


def local(features, row_weight, col_weight, conv_weight, conv_bias, dilations):
    row_local = jnp.dot(features, row_weight, preferred_element_type=jnp.float32).astype(
        jnp.bfloat16
    )
    col_local = jnp.dot(features, col_weight, preferred_element_type=jnp.float32).astype(
        jnp.bfloat16
    )
    row_all, col_all = (
        lax.all_gather(row_local, ("row", "col"), axis=0, tiled=True),
        lax.all_gather(col_local, ("row", "col"), axis=0, tiled=True),
    )
    return grid_plan(row_all, col_all, conv_weight, conv_bias, dilations)


def solution(mesh):
    placed = (P(("row", "col"), None), P(), P(), P(), P(), P())
    return jax.shard_map(
        local, mesh=mesh, in_specs=placed, out_specs=P(None, "row", "col"), check_vma=False
    )
```

profile of v0, /device:TPU:0, one launch (start us, length us, event | category | flops | bytes accessed | tf_op | source)
XLA Modules:
  0.0 860.1 jit_solution(7645530848305929042)
XLA Ops:
  0.0 1.3 fusion.32
  3.9 0.8 convolution_convert_fusion
  4.7 319.4 %all_gather.7 = bf16[1024,32]{1,0:T(8,128)(2,1)S(1)} all-gather(bf16[8,32]{1,0:T(8,128)(2,1)S(1)} %convolution_convert_fusion), channel_id=1, replica_groups=mesh['row'=16,'col'=8] {'row','col'}, dimensions={0}, use_global_device_ids=true | all-gather | bytes 66048 | tf_op jit(solution)/shard_map/all_gather | solution.py:145
  324.3 0.8 convolution_convert_fusion.1
  325.1 311.3 %all_gather.6 = bf16[1024,32]{1,0:T(8,128)(2,1)S(1)} all-gather(bf16[8,32]{1,0:T(8,128)(2,1)S(1)} %convolution_convert_fusion.1), channel_id=1, replica_groups=mesh['row'=16,'col'=8] {'row','col'}, dimensions={0}, use_global_device_ids=true | all-gather | bytes 66048 | tf_op jit(solution)/shard_map/all_gather | solution.py:144
  636.4 0.9 slice_bitcast_fusion
  637.7 0.8 slice_bitcast_fusion.6
  638.6 0.4 broadcast_multiply_fusion.1
  639.0 0.6 fusion.14
  639.6 3.6 constant_dynamic-slice_fusion.10
  643.2 0.5 maximum_bitcast_fusion
  643.7 0.7 fusion.11
  644.4 0.8 convolution_add_fusion.3
  645.2 1.3 fusion.21
  646.5 0.6 fusion.16
  647.0 14.7 %all_to_all.90 = bf16[64,64,128]{2,0,1:T(8,128)(2,1)} all-to-all(bf16[64,64,128]{2,0,1:T(8,128)(2,1)S(1)} %fusion.16), channel_id=1, replica_groups=mesh['row'=16,'col'=8] {'col'}, dimensions={1} | all-to-all | bytes 2097152 | tf_op jit(solution)/shard_map/all_to_all | solution.py:119
  661.7 2.1 copy.53
  663.9 2.3 reshape.124
  666.2 24.7 %all_to_all.91 = bf16[128,2,2048]{2,1,0:T(2,128)(2,1)} all-to-all(bf16[128,2,2048]{2,1,0:T(2,128)(2,1)} %reshape.124), channel_id=1, replica_groups=mesh['row'=16,'col'=8] {'row','col'}, dimensions={0} | all-to-all | bytes 2097152 | tf_op jit(solution)/shard_map/all_to_all | solution.py:120
  690.9 3.8 reshape.125
  694.7 0.4 copy.116
  695.1 1.4 copy.118
  696.5 2.7 reshape.126
  699.2 18.4 %all_to_all.92 = bf16[8,2,32768]{2,1,0:T(2,128)(2,1)S(1)} all-to-all(bf16[8,2,32768]{2,1,0:T(2,128)(2,1)} %reshape.126), channel_id=1, replica_groups=mesh['row'=16,'col'=8] {'col'}, dimensions={0} | all-to-all | bytes 2097152 | tf_op jit(solution)/shard_map/all_to_all | solution.py:123
  717.6 2.7 reshape.127
  720.3 2.4 copy.56
  722.7 0.4 broadcast_maximum_fusion
  723.2 1.3 collective-permute-start
  724.5 1.3 collective-permute-start.1
  725.8 4.2 collective-permute-done.1
  730.0 0.2 pad_maximum_fusion.2
  730.1 1.9 fusion.30
  732.1 2.6 copy.57
  734.7 2.7 collective-permute-start.2
  737.4 2.6 copy.58
  740.0 1.3 collective-permute-start.3
  743.5 0.7 copy.62
  744.3 0.7 copy.64
  745.0 0.7 copy.66
  745.7 2.9 copy.59
  748.6 2.9 copy.60
  751.5 3.5 pad_maximum_fusion.1
  755.0 6.6 constant_dynamic-slice_fusion.2
  761.6 2.5 fusion.4
  764.1 0.3 copy-done.10
  764.4 1.3 convolution_add_fusion.1
  765.7 0.2 copy-done.7
  766.0 0.3 copy-done.8
  766.3 1.2 fusion.24
  767.5 0.3 copy-done.3
  767.9 0.6 fusion.15
  768.4 19.1 %all_to_all.93 = bf16[64,64,128]{2,0,1:T(8,128)(2,1)S(1)} all-to-all(bf16[64,64,128]{2,0,1:T(8,128)(2,1)S(1)} %fusion.15), channel_id=1, replica_groups=mesh['row'=16,'col'=8] {'col'}, dimensions={1} | all-to-all | bytes 2097152 | tf_op jit(solution)/shard_map/all_to_all | solution.py:119
  787.5 2.0 copy.68
  789.6 3.9 reshape.128
  793.5 28.8 %all_to_all.94 = bf16[128,2,2048]{2,1,0:T(2,128)(2,1)S(1)} all-to-all(bf16[128,2,2048]{2,1,0:T(2,128)(2,1)S(1)} %reshape.128), channel_id=1, replica_groups=mesh['row'=16,'col'=8] {'row','col'}, dimensions={0} | all-to-all | bytes 2097152 | tf_op jit(solution)/shard_map/all_to_all | solution.py:120
  822.3 2.3 reshape.129
  824.6 2.0 copy.115
  826.6 2.7 copy.117
  829.2 3.4 reshape.130
  832.6 17.8 %all_to_all.95 = bf16[8,2,32768]{2,1,0:T(2,128)(2,1)S(1)} all-to-all(bf16[8,2,32768]{2,1,0:T(2,128)(2,1)S(1)} %reshape.130), channel_id=1, replica_groups=mesh['row'=16,'col'=8] {'col'}, dimensions={0} | all-to-all | bytes 2097152 | tf_op jit(solution)/shard_map/all_to_all | solution.py:123
  850.4 2.7 reshape.131
  853.1 3.4 copy.71
  856.5 2.0 fusion.18
  858.5 1.6 copy.72
  (37 shorter events, 0.6 us)
Async XLA Ops:
  0.0 3.9 copy-start
  722.7 7.4 copy-start.2
  723.1 6.8 copy-start.4
  723.2 2.6 collective-permute-start
  724.5 5.5 collective-permute-start.1
  734.7 11.0 %collective-permute-start.2 = (bf16[64,72,4]{1,0,2:T(8,128)(2,1)S(1)}, bf16[64,72,4]{1,0,2:T(8,128)(2,1)S(1)}, u32[]{:S(2)}, u32[]{:S(2)}) collective-permute-start(bf16[64,72,4]{1,0,2:T(8,128)(2,1)S(1)} %copy.57), channel_id=1, source_target_pairs={{0,1},{1,2},{2,3},{3,4},{4,5},{5,6},{6,7},{8,9},{9,10},{10,11},{11... | collective-permute-start | bytes 110600 | tf_op jit(solution)/shard_map/ppermute | solution.py:14
  740.0 8.5 collective-permute-start.3
  755.0 6.6 copy-start.13
  761.6 2.5 copy-start.5
  761.6 2.5 copy-start.9
  761.6 2.8 copy-start.10
  761.6 2.8 copy-start.12
  764.4 1.3 copy-start.6
  764.4 1.5 copy-start.7
  764.4 1.9 copy-start.8
  764.4 1.9 copy-start.11
  766.3 1.6 copy-start.3
  853.1 7.1 copy-start.1
where the time goes:
time: 861 us; the launch traced here: 860 us
  blocking collectives  754 us (88%)
  local copies, waits for them, and re-layouts  71.7 us (8%)
  matrix products  9.37 us (1%)
  other arithmetic  8.78 us (1%)
    all_gather x1, blocking collectives, local(): lax.all_gather(col_local, ('row', 'col'), axis=0, tiled=True)  319 us
    all_gather x1, blocking collectives, local(): lax.all_gather(row_local, ('row', 'col'), axis=0, tiled=True)  311 us
    all_to_all x2, blocking collectives, grid_layer(): lax.all_to_all(jnp.swapaxes(strips, 1, 2), ('row', 'col'), split_axis=1,...  53.5 us
    all_to_all x2, blocking collectives, grid_layer(): lax.all_to_all(turned, 'col', split_axis=2, concat_axis=1, tiled=True)  36.2 us
    all_to_all x2, blocking collectives, grid_layer(): lax.all_to_all(mixed_map, 'col', split_axis=1, concat_axis=2, tiled=True)  33.8 us
    unnamed x36, local copies, waits for them, and re-layouts  25 us
  transfers between devices with their start and end apart: 4, of which 1 were waited for; matrix products, arithmetic and copies ran while one was open for 1% of the time, Pallas kernels for 0%

commit v1 on v0

--- a/solution.py
+++ b/solution.py
@@ -142,7 +142,12 @@
     )
     row_all, col_all = (
         lax.all_gather(row_local, ("row", "col"), axis=0, tiled=True),
-        lax.all_gather(col_local, ("row", "col"), axis=0, tiled=True),
+        jnp.concatenate(
+            lax.all_to_all(
+                jnp.stack([col_local] * lax.axis_size(("row", "col"))), ("row", "col"), 0, 0
+            ),
+            axis=0,
+        ),
     )
     return grid_plan(row_all, col_all, conv_weight, conv_bias, dilations)
 

time: 861 us -> 561 us (0.65)
  blocking collectives: 754 us -> 441 us
  starting transfers between devices: 6.55 us -> 17.7 us
    all_gather x1 -> x0, blocking collectives: 319 us -> none  [local(): lax.all_gather(col_local, ('row', 'col'), axis=0, tiled=True)]
    all_to_all x0 -> x1, starting transfers between devices: none -> 11.2 us  [local(): lax.all_to_all(jnp.stack([col_local] * lax.axis_size(('row', 'col'))), ('...]
    unnamed x36 -> x38, local copies, waits for them, and re-layouts: 25 us -> 26.5 us
  transfers between devices with their start and end apart: 4 -> 5, of which waited for: 1 -> 1; matrix products, arithmetic and copies ran while one was open for 1% -> 2% of each run, Pallas kernels for 0% -> 0%
where the time goes in v1:
time: 561 us; the launch traced here: 560 us
  blocking collectives  441 us (79%)
  local copies, waits for them, and re-layouts  73.3 us (13%)
  starting transfers between devices  17.7 us (3%)
  matrix products  9.34 us (2%)
  other arithmetic  8.76 us (2%)
    all_gather x1, blocking collectives, local(): lax.all_gather(row_local, ('row', 'col'), axis=0, tiled=True)  318 us
    all_to_all x2, blocking collectives, grid_layer(): lax.all_to_all(jnp.swapaxes(strips, 1, 2), ('row', 'col'), split_axis=1,...  53.5 us
    all_to_all x2, blocking collectives, grid_layer(): lax.all_to_all(turned, 'col', split_axis=2, concat_axis=1, tiled=True)  36.2 us
    all_to_all x2, blocking collectives, grid_layer(): lax.all_to_all(mixed_map, 'col', split_axis=1, concat_axis=2, tiled=True)  33.4 us
    unnamed x38, local copies, waits for them, and re-layouts  26.5 us
  transfers between devices with their start and end apart: 5, of which 1 were waited for; matrix products, arithmetic and copies ran while one was open for 2% of the time, Pallas kernels for 0%

profile of v1, /device:TPU:0, one launch (start us, length us, event | category | flops | bytes accessed | tf_op | source)
XLA Modules:
  0.0 560.2 jit_solution(16438098275071531780)
XLA Ops:
  0.0 0.7 copy-done
  0.7 0.8 convolution_convert_fusion
  1.5 0.8 reshape.130
  2.4 11.2 %all-to-all-start = ((bf16[128,2,128]{2,1,0:T(2,128)(2,1)}), bf16[128,2,128]{2,1,0:T(2,128)(2,1)S(1)}, u32[]{:S(2)}, u32[]{:S(2)}) async-start(bf16[128,2,128]{2,1,0:T(2,128)(2,1)} %reshape.130), calls=%async_computation | async-start | bytes 131072 | tf_op jit(solution)/shard_map/all_to_all | solution.py:146
  13.6 1.3 fusion.32
  17.6 0.8 convolution_convert_fusion.1
  18.5 318.4 %all_gather.3 = bf16[1024,32]{1,0:T(8,128)(2,1)S(1)} all-gather(bf16[8,32]{1,0:T(8,128)(2,1)S(1)} %convolution_convert_fusion.1), channel_id=1, replica_groups=mesh['row'=16,'col'=8] {'row','col'}, dimensions={0}, use_global_device_ids=true | all-gather | bytes 66048 | tf_op jit(solution)/shard_map/all_gather | solution.py:144
  336.8 0.9 slice_bitcast_fusion
  338.1 0.8 slice_bitcast_fusion.6
  338.9 0.4 broadcast_multiply_fusion.1
  339.7 0.6 fusion.14
  340.3 3.6 constant_dynamic-slice_fusion.10
  343.9 0.5 maximum_bitcast_fusion
  344.4 0.7 fusion.11
  345.1 0.8 convolution_add_fusion.3
  345.9 1.3 fusion.21
  347.2 0.6 fusion.16
  347.7 14.3 %all_to_all.95 = bf16[64,64,128]{2,0,1:T(8,128)(2,1)} all-to-all(bf16[64,64,128]{2,0,1:T(8,128)(2,1)S(1)} %fusion.16), channel_id=1, replica_groups=mesh['row'=16,'col'=8] {'col'}, dimensions={1} | all-to-all | bytes 2097152 | tf_op jit(solution)/shard_map/all_to_all | solution.py:119
  362.0 2.1 copy.53
  364.1 2.3 reshape.132
  366.4 24.7 %all_to_all.96 = bf16[128,2,2048]{2,1,0:T(2,128)(2,1)} all-to-all(bf16[128,2,2048]{2,1,0:T(2,128)(2,1)} %reshape.132), channel_id=1, replica_groups=mesh['row'=16,'col'=8] {'row','col'}, dimensions={0} | all-to-all | bytes 2097152 | tf_op jit(solution)/shard_map/all_to_all | solution.py:120
  391.1 3.8 reshape.133
  394.9 0.4 copy.116
  395.3 1.4 copy.118
  396.6 2.7 reshape.134
  399.3 18.4 %all_to_all.97 = bf16[8,2,32768]{2,1,0:T(2,128)(2,1)S(1)} all-to-all(bf16[8,2,32768]{2,1,0:T(2,128)(2,1)} %reshape.134), channel_id=1, replica_groups=mesh['row'=16,'col'=8] {'col'}, dimensions={0} | all-to-all | bytes 2097152 | tf_op jit(solution)/shard_map/all_to_all | solution.py:123
  417.7 2.7 reshape.135
  420.4 2.4 copy.56
  422.9 0.4 broadcast_maximum_fusion
  423.3 1.3 collective-permute-start
  424.6 1.3 collective-permute-start.1
  425.9 4.2 collective-permute-done.1
  430.3 1.9 fusion.30
  432.2 2.6 copy.57
  434.9 2.7 collective-permute-start.2
  437.5 2.6 copy.58
  440.2 1.3 collective-permute-start.3
  443.7 0.7 copy.62
  444.4 0.7 copy.64
  445.1 0.7 copy.66
  445.8 2.9 copy.59
  448.7 2.9 copy.60
  451.6 3.5 pad_maximum_fusion.1
  455.1 6.6 %constant_dynamic-slice_fusion.2 = (bf16[64,64,128]{2,0,1:T(8,128)(2,1)}, bf16[64,64,128]{2,0,1:T(8,128)(2,1)}, bf16[64,64,128]{2,0,1:T(8,128)(2,1)}, bf16[64,64...) fusion(bf16[64,72,136]{2,0,1:T(8,128)(2,1)S(1)} %pad_maximum_fu, ...), kind=kLoop, calls=%fused_computation.62 | loop fusion | bytes 16777232 | tf_op jit(solution)/shard_map/dynamic_slice | solution.py:39
  461.8 2.5 fusion.4
  464.2 0.3 copy-done.10
  464.6 1.3 convolution_add_fusion.1
  466.1 0.3 copy-done.8
  466.4 1.2 fusion.24
  467.6 0.3 copy-done.3
  468.0 0.6 fusion.15
  468.5 19.1 %all_to_all.98 = bf16[64,64,128]{2,0,1:T(8,128)(2,1)S(1)} all-to-all(bf16[64,64,128]{2,0,1:T(8,128)(2,1)S(1)} %fusion.15), channel_id=1, replica_groups=mesh['row'=16,'col'=8] {'col'}, dimensions={1} | all-to-all | bytes 2097152 | tf_op jit(solution)/shard_map/all_to_all | solution.py:119
  487.7 2.0 copy.68
  489.7 3.9 reshape.136
  493.6 28.8 %all_to_all.99 = bf16[128,2,2048]{2,1,0:T(2,128)(2,1)S(1)} all-to-all(bf16[128,2,2048]{2,1,0:T(2,128)(2,1)S(1)} %reshape.136), channel_id=1, replica_groups=mesh['row'=16,'col'=8] {'row','col'}, dimensions={0} | all-to-all | bytes 2097152 | tf_op jit(solution)/shard_map/all_to_all | solution.py:120
  522.4 2.3 reshape.137
  524.7 2.0 copy.115
  526.6 2.7 copy.117
  529.3 3.4 reshape.138
  532.7 17.8 %all_to_all.100 = bf16[8,2,32768]{2,1,0:T(2,128)(2,1)S(1)} all-to-all(bf16[8,2,32768]{2,1,0:T(2,128)(2,1)S(1)} %reshape.138), channel_id=1, replica_groups=mesh['row'=16,'col'=8] {'col'}, dimensions={0} | all-to-all | bytes 2097152 | tf_op jit(solution)/shard_map/all_to_all | solution.py:123
  550.5 2.7 reshape.139
  553.1 3.4 copy.71
  556.6 2.0 fusion.18
  558.5 1.6 copy.72
  (41 shorter events, 1.3 us)
Async XLA Ops:
  0.0 0.7 copy-start
  2.4 336.9 %all-to-all-start = ((bf16[128,2,128]{2,1,0:T(2,128)(2,1)}), bf16[128,2,128]{2,1,0:T(2,128)(2,1)S(1)}, u32[]{:S(2)}, u32[]{:S(2)}) async-start(bf16[128,2,128]{2,1,0:T(2,128)(2,1)} %reshape.130), calls=%async_computation | async-start | bytes 131072 | tf_op jit(solution)/shard_map/all_to_all | solution.py:146
  422.8 7.4 %copy-start.2 = (f32[64,8,8,128]{3,0,1,2:T(8,128)}, f32[64,8,8,128]{3,0,1,2:T(8,128)S(1)}, u32[]{:S(2)}) copy-start(f32[64,8,8,128]{3,0,1,2:T(8,128)S(1)} %copy.56) | copy-start | bytes 6291460
  423.3 6.8 %copy-start.4 = (bf16[64,64,128]{2,0,1:T(8,128)(2,1)}, bf16[64,64,128]{2,0,1:T(8,128)(2,1)S(1)}, u32[]{:S(2)}) copy-start(bf16[64,64,128]{2,0,1:T(8,128)(2,1)S(1)} %broadcast_maximum_fusion) | copy-start | bytes 3145732
  423.3 2.6 collective-permute-start
  424.6 5.5 collective-permute-start.1
  434.9 10.9 %collective-permute-start.2 = (bf16[64,72,4]{1,0,2:T(8,128)(2,1)S(1)}, bf16[64,72,4]{1,0,2:T(8,128)(2,1)S(1)}, u32[]{:S(2)}, u32[]{:S(2)}) collective-permute-start(bf16[64,72,4]{1,0,2:T(8,128)(2,1)S(1)} %copy.57), channel_id=1, source_target_pairs={{0,1},{1,2},{2,3},{3,4},{4,5},{5,6},{6,7},{8,9},{9,10},{10,11},{11... | collective-permute-start | bytes 110600 | tf_op jit(solution)/shard_map/ppermute | solution.py:14
  440.2 8.5 %collective-permute-start.3 = (bf16[64,72,4]{1,0,2:T(8,128)(2,1)S(1)}, bf16[64,72,4]{1,0,2:T(8,128)(2,1)S(1)}, u32[]{:S(2)}, u32[]{:S(2)}) collective-permute-start(bf16[64,72,4]{1,0,2:T(8,128)(2,1)S(1)} %copy.58), channel_id=1, source_target_pairs={{1,0},{2,1},{3,2},{4,3},{5,4},{6,5},{7,6},{9,8},{10,9},{11,10},{12... | collective-permute-start | bytes 110600 | tf_op jit(solution)/shard_map/ppermute | solution.py:17
  455.1 6.6 %copy-start.13 = (bf16[64,3,64]{0,2,1:T(8,128)(2,1)S(1)}, bf16[64,3,64]{0,2,1:T(8,128)(2,1)}, u32[]{:S(2)}) copy-start(bf16[64,3,64]{0,2,1:T(8,128)(2,1)} %copy.62) | copy-start | bytes 73732
  461.7 2.5 copy-start.5
  461.7 2.5 copy-start.9
  461.7 2.8 copy-start.10
  461.7 2.8 copy-start.12
  464.5 1.3 copy-start.6
  464.5 1.5 copy-start.7
  464.5 1.9 copy-start.8
  464.5 1.9 copy-start.11
  466.4 1.6 copy-start.3
  553.1 7.0 %copy-start.1 = (bf16[128,32]{0,1:T(8,128)(2,1)S(1)}, bf16[128,32]{0,1:T(8,128)(2,1)}, u32[]{:S(2)}) copy-start(bf16[128,32]{0,1:T(8,128)(2,1)} %param.8) | copy-start | bytes 24580
